TPU v7x, 256 devices: a whole 4x4x8 slice. The times are simulated.
256 devices in a mesh: rows: 128 (over z, x, y_lo, core), grp: 2 (over y_hi).
Axes of the slice: x: 4, y: 4 (y_hi: 2, y_lo: 2; y = y_hi * 2 + y_lo), z: 8, core: 2. Of those that a mesh axis runs over, the one named last changes fastest.
Arguments:
- embeddings: bfloat16 [393216, 1024], P(('rows', 'grp')), may hold values from -6 to 6
- centroids: float32 [16384, 1024], P('rows', 'grp'), may hold values from -6 to 6
- block_lists: int32 [3072, 7], P(('rows', 'grp')), may hold values from -1 to 127, as said below
- block_counts: int32 [3072], P(('rows', 'grp')), may hold values from 1 to 7, as said below
Outputs:
- new_centroids: float32 [16384, 1024], P('rows', 'grp')
- evidence: float32 [393216], P(('rows', 'grp'))
Inputs may be any that keep to these rules, and one draw needn't show every extreme that they name: `block_lists`: row block b is held by rows index r = b // 24. The first entry of its list is r; the entries j < block_counts[b] are distinct centroid block ids within cyclic distance 3 of r (modulo 128); entries from block_counts[b] on are -1. `block_counts`: all row blocks of one rows index have counts within one of each other; in every draw some rows index has all its counts equal to 7.
All inputs are finite; a program needn't handle non-finite values.
Results may differ from a plain program's by a relative error of at most 0.012.
The roundings to bfloat16 on the way count: a program that leaves them out, or rounds other values in their place, can miss the bound.
Values may be sent and summed in bfloat16 or wider, within the bound.
A program may use at most 128 MiB of HBM per device.

v0:
```python
import jax
import jax.numpy as jnp
from jax import lax
from jax.sharding import PartitionSpec as P

D = 1024
RB = 128
W = 3
ITERS = 2


EPS = 1e-06
TAU = 20.0


def shifted(block, axis, distance):
    devices = range(lax.axis_size(axis))
    route = [((i - distance) % len(devices), i) for i in devices]
    return lax.ppermute(block, axis, route)


def normalize_rows(values):
    return values * lax.rsqrt(jnp.mean(values * values, axis=-1, keepdims=True) + EPS)


def renorm_shard(centroid_part):
    squares = jnp.sum(centroid_part * centroid_part, axis=1)
    totals = lax.psum(squares, "grp")
    return centroid_part * lax.rsqrt(totals / D + EPS)[:, None]


def fetch_window(low_copy):
    pieces = []
    own_block = lax.all_gather(low_copy, "grp", axis=1, tiled=True)
    for place in range(2 * W + 1):
        if place == W:
            pieces.append(own_block)
        else:
            pieces.append(shifted(own_block, "rows", W - place))
    return jnp.stack(pieces)


def return_sums(partial_value):
    collected = partial_value[W]
    for place in range(2 * W + 1):
        if place != W:
            collected = collected + shifted(
                partial_value[place].astype(jnp.bfloat16), "rows", place - W
            ).astype(jnp.float32)
    return lax.psum_scatter(
        collected.astype(jnp.bfloat16), "grp", scatter_dimension=1, tiled=True
    ).astype(jnp.float32)


def score_dense(unit_rows, window, listed):
    span, block_width, width = window.shape
    row_count = unit_rows.shape[0]
    group = min(512, row_count)
    groups = row_count // group
    per_group = group // RB
    flat = window.reshape(span * block_width, width)

    def one_group(carry, group_index):
        members = lax.dynamic_slice_in_dim(unit_rows, group_index * group, group)
        chosen = lax.dynamic_slice_in_dim(listed, group_index * per_group, per_group)
        scores = lax.dot_general(
            members, flat, (((1,), (1,)), ((), ())), preferred_element_type=jnp.float32
        ) * (TAU / D)
        grid = scores.reshape(per_group, RB, span, block_width)
        weights = jnp.where(chosen[:, None, :, None], jnp.exp(grid), 0.0)
        totals = jnp.sum(weights, axis=(2, 3))
        shares = (
            (weights / totals[:, :, None, None])
            .astype(jnp.bfloat16)
            .reshape(group, span * block_width)
        )
        contribution = lax.dot_general(
            shares, members, (((0,), (0,)), ((), ())), preferred_element_type=jnp.float32
        )
        return (carry + contribution, jnp.log(totals).reshape(group))

    start = jnp.zeros((span * block_width, width), jnp.float32)
    partial_value, logs = lax.scan(one_group, start, jnp.arange(groups))
    return (partial_value.reshape(span, block_width, width), logs.reshape(row_count))


def local(embeddings, centroids, block_lists, block_counts):
    row_rank = lax.axis_index("rows")
    block_total = lax.axis_size("rows")
    span = 2 * W + 1
    unit_rows = normalize_rows(embeddings.astype(jnp.float32)).astype(jnp.bfloat16)
    places = jnp.mod(block_lists - row_rank + W, block_total)
    slot_index = jnp.arange(span, dtype=jnp.int32)
    in_count = slot_index[None, :] < block_counts[:, None]
    listed = jnp.any(
        (places[:, :, None] == slot_index[None, None, :]) & in_count[:, :, None], axis=1
    )
    current = renorm_shard(centroids)
    evidence = jnp.zeros((unit_rows.shape[0],), jnp.float32)
    for rounds in range(ITERS):
        low_copy = current.astype(jnp.bfloat16)
        window = fetch_window(low_copy)
        partial_value, evidence = score_dense(unit_rows, window, listed)
        current = renorm_shard(return_sums(partial_value))
    return (current, evidence)


def solution(mesh):
    return jax.shard_map(
        local,
        mesh=mesh,
        in_specs=(
            P(("rows", "grp"), None),
            P("rows", "grp"),
            P(("rows", "grp"), None),
            P(("rows", "grp")),
        ),
        out_specs=(P("rows", "grp"), P(("rows", "grp"))),
        check_vma=False,
    )
```

profile of v0, /device:TPU:1, one launch (start us, length us, event | category | flops | bytes accessed | tf_op | source)
XLA Modules:
  0.0 281.6 jit_solution(2781548913164659497)
XLA Ops:
  8.3 6.1 %psum.21 = f32[128]{0:T(128)S(1)} all-reduce(f32[128]{0:T(128)S(1)} %multiply_reduce_fusion), channel_id=1, replica_groups=mesh['rows'=128,'grp'=2] {'grp'}, use_global_device_ids=true, to_apply=%region_3.4 | all-reduce | flops 128 | bytes 1024 | tf_op jit(solution)/shard_map/psum | solution.py:28
  15.4 6.1 %all_gather.6 = bf16[128,1024]{1,0:T(8,128)(2,1)S(1)} all-gather(bf16[128,512]{1,0:T(8,128)(2,1)S(1)} %multiply_convert_fusion), channel_id=1, replica_groups=mesh['rows'=128,'grp'=2] {'grp'}, dimensions={1}, use_global_device_ids=true | all-gather | bytes 393216 | tf_op jit(solution)/shard_map/all_gather | solution.py:34
  21.5 4.1 %collective-permute-start = (bf16[128,1024]{1,0:T(8,128)(2,1)S(1)}, bf16[128,1024]{1,0:T(8,128)(2,1)S(1)}, u32[]{:S(2)}, u32[]{:S(2)}) collective-permute-start(bf16[128,1024]{1,0:T(8,128)(2,1)S(1)} %all_gather.6), channel_id=1, source_target_pairs={{250,0},{252,2},{254,4},{0,6},{2,8},{4,10},{6,12},{8,14},{10,16},{... | collective-permute-start | bytes 786440 | tf_op jit(solution)/shard_map/ppermute | solution.py:19
  27.5 6.0 %collective-permute-start.4 = (bf16[128,1024]{1,0:T(8,128)(2,1)S(1)}, bf16[128,1024]{1,0:T(8,128)(2,1)S(1)}, u32[]{:S(2)}, u32[]{:S(2)}) collective-permute-start(bf16[128,1024]{1,0:T(8,128)(2,1)S(1)} %all_gather.6), channel_id=1, source_target_pairs={{4,0},{6,2},{8,4},{10,6},{12,8},{14,10},{16,12},{18,14},{20,16},{2... | collective-permute-start | bytes 786440 | tf_op jit(solution)/shard_map/ppermute | solution.py:19
  33.4 2.6 fusion.10
  36.1 2.3 fusion.11
  38.4 2.1 collective-permute-done
  40.5 2.5 collective-permute-start.5
  44.1 5.3 %collective-permute-done.2 = bf16[128,1024]{1,0:T(8,128)(2,1)S(1)} collective-permute-done((bf16[128,1024]{1,0:T(8,128)(2,1)S(1)}, bf16[128,1024]{1,0:T(8,128)(2,1)S(1)}, u32[]{:S(2)}, u32[]{:S(2)}) %collective-permute-start.2) | collective-permute-done | bytes 262176 | tf_op jit(solution)/shard_map/ppermute | solution.py:19
  49.6 37.7 %while.24 = (s32[]{:T(128)}, f32[896,1024]{1,0:T(8,128)}, s32[3]{0:T(128)S(1)}, pred[12,7]{0,1:T(8,128)(4,1)S(1)}, bf16[1536,1024]{1,0:T(8,128)(2,1)}, /*index=5...) while((s32[]{:T(128)}, f32[896,1024]{1,0:T(8,128)}, ...), condition=%wide.region_6.7_spmd.clone, body=%wide.region_4.6_spmd.clone.sunk | while | flops 1883176448 | bytes 17699144 | solution.py:83
  52.7 3.9 %fusion.32 = (f32[512]{0:T(512)S(1)}, f32[512,896]{1,0:T(8,128)}) fusion(pred[512,896]{1,0:T(32,128)(4,1)S(1)} %copy.23, bf16[896,1024]{1,0:T(8,128)(2,1)S(1)} %get-tuple-element.279, bf16[1536,1024]{1,0:T(8,128)(2,1)} %get-tuple-element.278, s32[]{:T(128)S(6)} %select_n.44), kind=kOutput, calls=%fused_computation.61.clone.1 | convolution fusion | flops 940899840 | bytes 5179396 | tf_op jit(solution)/shard_map/while/body/eval_jaxpr/dot_general | solution.py:66
  56.6 4.8 %select_add_fusion.4 = f32[896,1024]{1,0:T(8,128)} fusion(f32[896,1024]{1,0:T(8,128)} %get-tuple-element.263, pred[]{:T(512)S(6)} %compare.7, bf16[1536,1024]{1,0:T(8,128)(2,1)} %get-tuple-element.278, s32[]{:T(128)S(6)} %select_n.44, f32[512,896]{1,0:T(8,128)} %get-tuple-element.239, f32[512]{0:T(512)S(1)} %get-tuple-element.240), kind=kOutput, calls=%fused_computation.clone.1 | convolution fusion | flops 942276608 | bytes 10225669 | tf_op jit(solution)/shard_map/while/body/eval_jaxpr/dot_general | solution.py:77
  64.5 3.9 %fusion.32 = (f32[512]{0:T(512)S(1)}, f32[512,896]{1,0:T(8,128)}) fusion(pred[512,896]{1,0:T(32,128)(4,1)S(1)} %copy.23, bf16[896,1024]{1,0:T(8,128)(2,1)S(1)} %get-tuple-element.279, bf16[1536,1024]{1,0:T(8,128)(2,1)} %get-tuple-element.278, s32[]{:T(128)S(6)} %select_n.44), kind=kOutput, calls=%fused_computation.61.clone.1 | convolution fusion | flops 940899840 | bytes 5179396 | tf_op jit(solution)/shard_map/while/body/eval_jaxpr/dot_general | solution.py:66
  68.4 5.9 %select_add_fusion.4 = f32[896,1024]{1,0:T(8,128)} fusion(f32[896,1024]{1,0:T(8,128)} %get-tuple-element.263, pred[]{:T(512)S(6)} %compare.7, bf16[1536,1024]{1,0:T(8,128)(2,1)} %get-tuple-element.278, s32[]{:T(128)S(6)} %select_n.44, f32[512,896]{1,0:T(8,128)} %get-tuple-element.239, f32[512]{0:T(512)S(1)} %get-tuple-element.240), kind=kOutput, calls=%fused_computation.clone.1 | convolution fusion | flops 942276608 | bytes 10225669 | tf_op jit(solution)/shard_map/while/body/eval_jaxpr/dot_general | solution.py:77
  77.4 3.9 %fusion.32 = (f32[512]{0:T(512)S(1)}, f32[512,896]{1,0:T(8,128)}) fusion(pred[512,896]{1,0:T(32,128)(4,1)S(1)} %copy.23, bf16[896,1024]{1,0:T(8,128)(2,1)S(1)} %get-tuple-element.279, bf16[1536,1024]{1,0:T(8,128)(2,1)} %get-tuple-element.278, s32[]{:T(128)S(6)} %select_n.44), kind=kOutput, calls=%fused_computation.61.clone.1 | convolution fusion | flops 940899840 | bytes 5179396 | tf_op jit(solution)/shard_map/while/body/eval_jaxpr/dot_general | solution.py:66
  81.3 5.9 %select_add_fusion.4 = f32[896,1024]{1,0:T(8,128)} fusion(f32[896,1024]{1,0:T(8,128)} %get-tuple-element.263, pred[]{:T(512)S(6)} %compare.7, bf16[1536,1024]{1,0:T(8,128)(2,1)} %get-tuple-element.278, s32[]{:T(128)S(6)} %select_n.44, f32[512,896]{1,0:T(8,128)} %get-tuple-element.239, f32[512]{0:T(512)S(1)} %get-tuple-element.240), kind=kOutput, calls=%fused_computation.clone.1 | convolution fusion | flops 942276608 | bytes 10225669 | tf_op jit(solution)/shard_map/while/body/eval_jaxpr/dot_general | solution.py:77
  87.3 2.3 convert.16
  89.7 2.1 collective-permute-start.10
  92.6 6.6 %collective-permute-start.6 = (bf16[128,1024]{1,0:T(8,128)(2,1)S(1)}, bf16[128,1024]{1,0:T(8,128)(2,1)S(1)}, u32[]{:S(2)}, u32[]{:S(2)}) collective-permute-start(bf16[128,1024]{1,0:T(8,128)(2,1)S(1)} %get-tuple-element.156), channel_id=1, source_target_pairs={{6,0},{8,2},{10,4},{12,6},{14,8},{16,10},{18,12},{20,14},{22,16},{... | collective-permute-start | bytes 786440 | tf_op jit(solution)/shard_map/ppermute | solution.py:19
  101.3 2.9 %collective-permute-done.10 = bf16[128,1024]{1,0:T(8,128)(2,1)S(1)} collective-permute-done((bf16[128,1024]{1,0:T(8,128)(2,1)S(1)}, bf16[128,1024]{1,0:T(8,128)(2,1)S(1)}, u32[]{:S(2)}, u32[]{:S(2)}) %collective-permute-start.10) | collective-permute-done | bytes 262176 | tf_op jit(solution)/shard_map/ppermute | solution.py:19
  104.2 7.5 %collective-permute-start.9 = (bf16[128,1024]{1,0:T(8,128)(2,1)S(1)}, bf16[128,1024]{1,0:T(8,128)(2,1)S(1)}, u32[]{:S(2)}, u32[]{:S(2)}) collective-permute-start(bf16[128,1024]{1,0:T(8,128)(2,1)S(1)} %get-tuple-element.159), channel_id=1, source_target_pairs={{254,0},{0,2},{2,4},{4,6},{6,8},{8,10},{10,12},{12,14},{14,16},{16... | collective-permute-start | bytes 786440 | tf_op jit(solution)/shard_map/ppermute | solution.py:19
  111.7 1.9 collective-permute-done.7
  113.6 2.6 collective-permute-done.8
  116.2 2.0 add_convert_fusion.1
  118.3 19.5 %reduce-scatter.3.cloned.1.call-done = bf16[128,512]{1,0:T(8,128)(2,1)} async-done(((bf16[128,1024]{1,0:T(8,128)(2,1)}), bf16[128,512]{1,0:T(8,128)(2,1)}) %reduce-scatter.3.cloned.1.call-update) | async-done | bytes 131088 | tf_op jit(solution)/shard_map/reduce_scatter | solution.py:50
  138.8 5.3 %psum.22 = f32[128]{0:T(128)S(1)} all-reduce(f32[128]{0:T(128)S(1)} %fusion.12), channel_id=1, replica_groups=mesh['rows'=128,'grp'=2] {'grp'}, use_global_device_ids=true, to_apply=%region_9.10 | all-reduce | flops 128 | bytes 1024 | tf_op jit(solution)/shard_map/psum | solution.py:28
  145.1 6.0 %all_gather.7 = bf16[128,1024]{1,0:T(8,128)(2,1)S(1)} all-gather(bf16[128,512]{1,0:T(8,128)(2,1)S(1)} %fusion.13), channel_id=1, replica_groups=mesh['rows'=128,'grp'=2] {'grp'}, dimensions={1}, use_global_device_ids=true | all-gather | bytes 393216 | tf_op jit(solution)/shard_map/all_gather | solution.py:34
  151.1 4.0 %collective-permute-start.12 = (bf16[128,1024]{1,0:T(8,128)(2,1)S(1)}, bf16[128,1024]{1,0:T(8,128)(2,1)S(1)}, u32[]{:S(2)}, u32[]{:S(2)}) collective-permute-start(bf16[128,1024]{1,0:T(8,128)(2,1)S(1)} %all_gather.7), channel_id=1, source_target_pairs={{250,0},{252,2},{254,4},{0,6},{2,8},{4,10},{6,12},{8,14},{10,16},{... | collective-permute-start | bytes 786440 | tf_op jit(solution)/shard_map/ppermute | solution.py:19
  156.6 4.7 %collective-permute-start.16 = (bf16[128,1024]{1,0:T(8,128)(2,1)S(1)}, bf16[128,1024]{1,0:T(8,128)(2,1)S(1)}, u32[]{:S(2)}, u32[]{:S(2)}) collective-permute-start(bf16[128,1024]{1,0:T(8,128)(2,1)S(1)} %all_gather.7), channel_id=1, source_target_pairs={{4,0},{6,2},{8,4},{10,6},{12,8},{14,10},{16,12},{18,14},{20,16},{2... | collective-permute-start | bytes 786440 | tf_op jit(solution)/shard_map/ppermute | solution.py:19
  161.3 4.7 %collective-permute-done.12 = bf16[128,1024]{1,0:T(8,128)(2,1)S(1)} collective-permute-done((bf16[128,1024]{1,0:T(8,128)(2,1)S(1)}, bf16[128,1024]{1,0:T(8,128)(2,1)S(1)}, u32[]{:S(2)}, u32[]{:S(2)}) %collective-permute-start.12) | collective-permute-done | bytes 262176 | tf_op jit(solution)/shard_map/ppermute | solution.py:19
  167.7 4.8 %collective-permute-done.13 = bf16[128,1024]{1,0:T(8,128)(2,1)S(1)} collective-permute-done((bf16[128,1024]{1,0:T(8,128)(2,1)S(1)}, bf16[128,1024]{1,0:T(8,128)(2,1)S(1)}, u32[]{:S(2)}, u32[]{:S(2)}) %collective-permute-start.13) | collective-permute-done | bytes 262176 | tf_op jit(solution)/shard_map/ppermute | solution.py:19
  172.5 4.7 %collective-permute-done.14 = bf16[128,1024]{1,0:T(8,128)(2,1)S(1)} collective-permute-done((bf16[128,1024]{1,0:T(8,128)(2,1)S(1)}, bf16[128,1024]{1,0:T(8,128)(2,1)S(1)}, u32[]{:S(2)}, u32[]{:S(2)}) %collective-permute-start.14) | collective-permute-done | bytes 262176 | tf_op jit(solution)/shard_map/ppermute | solution.py:19
  177.4 37.8 %while.25 = (s32[]{:T(128)}, f32[896,1024]{1,0:T(8,128)}, f32[3,512]{1,0:T(4,128)S(1)}, s32[3]{0:T(128)S(1)}, pred[12,7]{0,1:T(8,128)(4,1)S(1)}, /*index=5*/bf16...) while((s32[]{:T(128)}, f32[896,1024]{1,0:T(8,128)}, ...), condition=%wide.region_12.13_spmd.clone, body=%wide.region_10.12_spmd.clone.sunk | while | flops 1883176448 | bytes 17707348 | solution.py:83
  180.5 3.9 %fusion.35 = (f32[512]{0:T(512)S(1)}, f32[512,896]{1,0:T(8,128)}) fusion(pred[512,896]{1,0:T(32,128)(4,1)S(1)} %copy.25, bf16[896,1024]{1,0:T(8,128)(2,1)S(1)} %get-tuple-element.318, bf16[1536,1024]{1,0:T(8,128)(2,1)} %get-tuple-element.317, s32[]{:T(128)S(6)} %select_n.46), kind=kOutput, calls=%fused_computation.62.clone.1 | convolution fusion | flops 940899840 | bytes 5179396 | tf_op jit(solution)/shard_map/while/body/eval_jaxpr/dot_general | solution.py:66
  184.4 4.8 %select_add_fusion.5 = f32[896,1024]{1,0:T(8,128)} fusion(f32[896,1024]{1,0:T(8,128)} %get-tuple-element.300, pred[]{:T(512)S(6)} %compare.8, bf16[1536,1024]{1,0:T(8,128)(2,1)} %get-tuple-element.317, s32[]{:T(128)S(6)} %select_n.46, f32[512,896]{1,0:T(8,128)} %get-tuple-element.248, f32[512]{0:T(512)S(1)} %get-tuple-element.249), kind=kOutput, calls=%fused_computation.10.clone.1 | convolution fusion | flops 942276608 | bytes 10225669 | tf_op jit(solution)/shard_map/while/body/eval_jaxpr/dot_general | solution.py:77
  192.4 3.9 %fusion.35 = (f32[512]{0:T(512)S(1)}, f32[512,896]{1,0:T(8,128)}) fusion(pred[512,896]{1,0:T(32,128)(4,1)S(1)} %copy.25, bf16[896,1024]{1,0:T(8,128)(2,1)S(1)} %get-tuple-element.318, bf16[1536,1024]{1,0:T(8,128)(2,1)} %get-tuple-element.317, s32[]{:T(128)S(6)} %select_n.46), kind=kOutput, calls=%fused_computation.62.clone.1 | convolution fusion | flops 940899840 | bytes 5179396 | tf_op jit(solution)/shard_map/while/body/eval_jaxpr/dot_general | solution.py:66
  196.3 5.9 %select_add_fusion.5 = f32[896,1024]{1,0:T(8,128)} fusion(f32[896,1024]{1,0:T(8,128)} %get-tuple-element.300, pred[]{:T(512)S(6)} %compare.8, bf16[1536,1024]{1,0:T(8,128)(2,1)} %get-tuple-element.317, s32[]{:T(128)S(6)} %select_n.46, f32[512,896]{1,0:T(8,128)} %get-tuple-element.248, f32[512]{0:T(512)S(1)} %get-tuple-element.249), kind=kOutput, calls=%fused_computation.10.clone.1 | convolution fusion | flops 942276608 | bytes 10225669 | tf_op jit(solution)/shard_map/while/body/eval_jaxpr/dot_general | solution.py:77
  205.3 3.9 %fusion.35 = (f32[512]{0:T(512)S(1)}, f32[512,896]{1,0:T(8,128)}) fusion(pred[512,896]{1,0:T(32,128)(4,1)S(1)} %copy.25, bf16[896,1024]{1,0:T(8,128)(2,1)S(1)} %get-tuple-element.318, bf16[1536,1024]{1,0:T(8,128)(2,1)} %get-tuple-element.317, s32[]{:T(128)S(6)} %select_n.46), kind=kOutput, calls=%fused_computation.62.clone.1 | convolution fusion | flops 940899840 | bytes 5179396 | tf_op jit(solution)/shard_map/while/body/eval_jaxpr/dot_general | solution.py:66
  209.2 5.9 %select_add_fusion.5 = f32[896,1024]{1,0:T(8,128)} fusion(f32[896,1024]{1,0:T(8,128)} %get-tuple-element.300, pred[]{:T(512)S(6)} %compare.8, bf16[1536,1024]{1,0:T(8,128)(2,1)} %get-tuple-element.317, s32[]{:T(128)S(6)} %select_n.46, f32[512,896]{1,0:T(8,128)} %get-tuple-element.248, f32[512]{0:T(512)S(1)} %get-tuple-element.249), kind=kOutput, calls=%fused_computation.10.clone.1 | convolution fusion | flops 942276608 | bytes 10225669 | tf_op jit(solution)/shard_map/while/body/eval_jaxpr/dot_general | solution.py:77
  215.2 2.3 convert.17
  217.7 7.3 %collective-permute-start.18 = (bf16[128,1024]{1,0:T(8,128)(2,1)S(1)}, bf16[128,1024]{1,0:T(8,128)(2,1)S(1)}, u32[]{:S(2)}, u32[]{:S(2)}) collective-permute-start(bf16[128,1024]{1,0:T(8,128)(2,1)S(1)} %get-tuple-element.150), channel_id=1, source_target_pairs={{6,0},{8,2},{10,4},{12,6},{14,8},{16,10},{18,12},{20,14},{22,16},{... | collective-permute-start | bytes 786440 | tf_op jit(solution)/shard_map/ppermute | solution.py:19
  226.4 1.7 collective-permute-start.21
  229.1 2.1 collective-permute-done.18
  231.2 15.8 %collective-permute-done.19 = bf16[128,1024]{1,0:T(8,128)(2,1)S(1)} collective-permute-done((bf16[128,1024]{1,0:T(8,128)(2,1)S(1)}, bf16[128,1024]{1,0:T(8,128)(2,1)S(1)}, u32[]{:S(2)}, u32[]{:S(2)}) %collective-permute-start.19) | collective-permute-done | bytes 262176 | tf_op jit(solution)/shard_map/ppermute | solution.py:19
  247.6 2.0 add_convert_fusion
  250.3 16.5 %reduce-scatter.5.cloned.1.call-done = bf16[128,512]{1,0:T(8,128)(2,1)} async-done(((bf16[128,1024]{1,0:T(8,128)(2,1)}), bf16[128,512]{1,0:T(8,128)(2,1)}) %reduce-scatter.5.cloned.1.call-update) | async-done | bytes 131088 | tf_op jit(solution)/shard_map/reduce_scatter | solution.py:50
  267.8 5.3 %psum.23 = f32[128]{0:T(128)S(1)} all-reduce(f32[128]{0:T(128)S(1)} %fusion.14), channel_id=1, replica_groups=mesh['rows'=128,'grp'=2] {'grp'}, use_global_device_ids=true, to_apply=%region_15.16 | all-reduce | flops 128 | bytes 1024 | tf_op jit(solution)/shard_map/psum | solution.py:28
  273.1 1.7 convert_multiply_fusion.2
  (108 shorter events, 28.9 us)
Async XLA Ops:
  7.2 130.6 %reduce-scatter.3.cloned.1.call-start = ((), (), s32[]{:S(2)}) async-start(), calls=%async_computation.2 | async-start | bytes 393216 | tf_op jit(solution)/shard_map/reduce_scatter | solution.py:50
  15.4 20.7 %copy-start = (bf16[1536,1024]{1,0:T(8,128)(2,1)S(1)}, bf16[1536,1024]{1,0:T(8,128)(2,1)}, u32[]{:S(2)}) copy-start(bf16[1536,1024]{1,0:T(8,128)(2,1)} %param.8) | copy-start | bytes 9437188
  21.5 18.9 %collective-permute-start = (bf16[128,1024]{1,0:T(8,128)(2,1)S(1)}, bf16[128,1024]{1,0:T(8,128)(2,1)S(1)}, u32[]{:S(2)}, u32[]{:S(2)}) collective-permute-start(bf16[128,1024]{1,0:T(8,128)(2,1)S(1)} %all_gather.6), channel_id=1, source_target_pairs={{250,0},{252,2},{254,4},{0,6},{2,8},{4,10},{6,12},{8,14},{10,16},{... | collective-permute-start | bytes 786440 | tf_op jit(solution)/shard_map/ppermute | solution.py:19
  25.7 18.4 %collective-permute-start.1 = (bf16[128,1024]{1,0:T(8,128)(2,1)S(1)}, bf16[128,1024]{1,0:T(8,128)(2,1)S(1)}, u32[]{:S(2)}, u32[]{:S(2)}) collective-permute-start(bf16[128,1024]{1,0:T(8,128)(2,1)S(1)} %all_gather.6), channel_id=1, source_target_pairs={{252,0},{254,2},{0,4},{2,6},{4,8},{6,10},{8,12},{10,14},{12,16},{1... | collective-permute-start | bytes 786440 | tf_op jit(solution)/shard_map/ppermute | solution.py:19
  27.0 22.5 %collective-permute-start.2 = (bf16[128,1024]{1,0:T(8,128)(2,1)S(1)}, bf16[128,1024]{1,0:T(8,128)(2,1)S(1)}, u32[]{:S(2)}, u32[]{:S(2)}) collective-permute-start(bf16[128,1024]{1,0:T(8,128)(2,1)S(1)} %all_gather.6), channel_id=1, source_target_pairs={{254,0},{0,2},{2,4},{4,6},{6,8},{8,10},{10,12},{12,14},{14,16},{16... | collective-permute-start | bytes 786440 | tf_op jit(solution)/shard_map/ppermute | solution.py:19
  27.1 22.4 %collective-permute-start.3 = (bf16[128,1024]{1,0:T(8,128)(2,1)S(1)}, bf16[128,1024]{1,0:T(8,128)(2,1)S(1)}, u32[]{:S(2)}, u32[]{:S(2)}) collective-permute-start(bf16[128,1024]{1,0:T(8,128)(2,1)S(1)} %all_gather.6), channel_id=1, source_target_pairs={{2,0},{4,2},{6,4},{8,6},{10,8},{12,10},{14,12},{16,14},{18,16},{20... | collective-permute-start | bytes 786440 | tf_op jit(solution)/shard_map/ppermute | solution.py:19
  27.5 22.1 %collective-permute-start.4 = (bf16[128,1024]{1,0:T(8,128)(2,1)S(1)}, bf16[128,1024]{1,0:T(8,128)(2,1)S(1)}, u32[]{:S(2)}, u32[]{:S(2)}) collective-permute-start(bf16[128,1024]{1,0:T(8,128)(2,1)S(1)} %all_gather.6), channel_id=1, source_target_pairs={{4,0},{6,2},{8,4},{10,6},{12,8},{14,10},{16,12},{18,14},{20,16},{2... | collective-permute-start | bytes 786440 | tf_op jit(solution)/shard_map/ppermute | solution.py:19
  36.0 2.3 copy-start.1
  36.1 2.3 copy-start.2
  40.5 9.1 %collective-permute-start.5 = (bf16[128,1024]{1,0:T(8,128)(2,1)S(1)}, bf16[128,1024]{1,0:T(8,128)(2,1)S(1)}, u32[]{:S(2)}, u32[]{:S(2)}) collective-permute-start(bf16[128,1024]{1,0:T(8,128)(2,1)S(1)} %all_gather.6), channel_id=1, source_target_pairs={{6,0},{8,2},{10,4},{12,6},{14,8},{16,10},{18,12},{20,14},{22,16},{... | collective-permute-start | bytes 786440 | tf_op jit(solution)/shard_map/ppermute | solution.py:19
  89.7 14.4 %collective-permute-start.10 = (bf16[128,1024]{1,0:T(8,128)(2,1)S(1)}, bf16[128,1024]{1,0:T(8,128)(2,1)S(1)}, u32[]{:S(2)}, u32[]{:S(2)}) collective-permute-start(bf16[128,1024]{1,0:T(8,128)(2,1)S(1)} %get-tuple-element.158), channel_id=1, source_target_pairs={{252,0},{254,2},{0,4},{2,6},{4,8},{6,10},{8,12},{10,14},{12,16},{1... | collective-permute-start | bytes 786440 | tf_op jit(solution)/shard_map/ppermute | solution.py:19
  91.9 19.8 %collective-permute-start.11 = (bf16[128,1024]{1,0:T(8,128)(2,1)S(1)}, bf16[128,1024]{1,0:T(8,128)(2,1)S(1)}, u32[]{:S(2)}, u32[]{:S(2)}) collective-permute-start(bf16[128,1024]{1,0:T(8,128)(2,1)S(1)} %get-tuple-element.157), channel_id=1, source_target_pairs={{250,0},{252,2},{254,4},{0,6},{2,8},{4,10},{6,12},{8,14},{10,16},{... | collective-permute-start | bytes 786440 | tf_op jit(solution)/shard_map/ppermute | solution.py:19
  92.6 19.2 %collective-permute-start.6 = (bf16[128,1024]{1,0:T(8,128)(2,1)S(1)}, bf16[128,1024]{1,0:T(8,128)(2,1)S(1)}, u32[]{:S(2)}, u32[]{:S(2)}) collective-permute-start(bf16[128,1024]{1,0:T(8,128)(2,1)S(1)} %get-tuple-element.156), channel_id=1, source_target_pairs={{6,0},{8,2},{10,4},{12,6},{14,8},{16,10},{18,12},{20,14},{22,16},{... | collective-permute-start | bytes 786440 | tf_op jit(solution)/shard_map/ppermute | solution.py:19
  99.2 14.5 %collective-permute-start.7 = (bf16[128,1024]{1,0:T(8,128)(2,1)S(1)}, bf16[128,1024]{1,0:T(8,128)(2,1)S(1)}, u32[]{:S(2)}, u32[]{:S(2)}) collective-permute-start(bf16[128,1024]{1,0:T(8,128)(2,1)S(1)} %get-tuple-element.161), channel_id=1, source_target_pairs={{4,0},{6,2},{8,4},{10,6},{12,8},{14,10},{16,12},{18,14},{20,16},{2... | collective-permute-start | bytes 786440 | tf_op jit(solution)/shard_map/ppermute | solution.py:19
  100.2 16.0 %collective-permute-start.8 = (bf16[128,1024]{1,0:T(8,128)(2,1)S(1)}, bf16[128,1024]{1,0:T(8,128)(2,1)S(1)}, u32[]{:S(2)}, u32[]{:S(2)}) collective-permute-start(bf16[128,1024]{1,0:T(8,128)(2,1)S(1)} %get-tuple-element.160), channel_id=1, source_target_pairs={{2,0},{4,2},{6,4},{8,6},{10,8},{12,10},{14,12},{16,14},{18,16},{20... | collective-permute-start | bytes 786440 | tf_op jit(solution)/shard_map/ppermute | solution.py:19
  104.2 12.0 %collective-permute-start.9 = (bf16[128,1024]{1,0:T(8,128)(2,1)S(1)}, bf16[128,1024]{1,0:T(8,128)(2,1)S(1)}, u32[]{:S(2)}, u32[]{:S(2)}) collective-permute-start(bf16[128,1024]{1,0:T(8,128)(2,1)S(1)} %get-tuple-element.159), channel_id=1, source_target_pairs={{254,0},{0,2},{2,4},{4,6},{6,8},{8,10},{10,12},{12,14},{14,16},{16... | collective-permute-start | bytes 786440 | tf_op jit(solution)/shard_map/ppermute | solution.py:19
  118.2 148.5 %reduce-scatter.5.cloned.1.call-start = ((), (), s32[]{:S(2)}) async-start(), calls=%async_computation.3 | async-start | bytes 393216 | tf_op jit(solution)/shard_map/reduce_scatter | solution.py:50
  151.1 14.9 %collective-permute-start.12 = (bf16[128,1024]{1,0:T(8,128)(2,1)S(1)}, bf16[128,1024]{1,0:T(8,128)(2,1)S(1)}, u32[]{:S(2)}, u32[]{:S(2)}) collective-permute-start(bf16[128,1024]{1,0:T(8,128)(2,1)S(1)} %all_gather.7), channel_id=1, source_target_pairs={{250,0},{252,2},{254,4},{0,6},{2,8},{4,10},{6,12},{8,14},{10,16},{... | collective-permute-start | bytes 786440 | tf_op jit(solution)/shard_map/ppermute | solution.py:19
  155.1 17.4 %collective-permute-start.13 = (bf16[128,1024]{1,0:T(8,128)(2,1)S(1)}, bf16[128,1024]{1,0:T(8,128)(2,1)S(1)}, u32[]{:S(2)}, u32[]{:S(2)}) collective-permute-start(bf16[128,1024]{1,0:T(8,128)(2,1)S(1)} %all_gather.7), channel_id=1, source_target_pairs={{252,0},{254,2},{0,4},{2,6},{4,8},{6,10},{8,12},{10,14},{12,16},{1... | collective-permute-start | bytes 786440 | tf_op jit(solution)/shard_map/ppermute | solution.py:19
  155.5 21.8 %collective-permute-start.14 = (bf16[128,1024]{1,0:T(8,128)(2,1)S(1)}, bf16[128,1024]{1,0:T(8,128)(2,1)S(1)}, u32[]{:S(2)}, u32[]{:S(2)}) collective-permute-start(bf16[128,1024]{1,0:T(8,128)(2,1)S(1)} %all_gather.7), channel_id=1, source_target_pairs={{254,0},{0,2},{2,4},{4,6},{6,8},{8,10},{10,12},{12,14},{14,16},{16... | collective-permute-start | bytes 786440 | tf_op jit(solution)/shard_map/ppermute | solution.py:19
  156.6 20.7 %collective-permute-start.15 = (bf16[128,1024]{1,0:T(8,128)(2,1)S(1)}, bf16[128,1024]{1,0:T(8,128)(2,1)S(1)}, u32[]{:S(2)}, u32[]{:S(2)}) collective-permute-start(bf16[128,1024]{1,0:T(8,128)(2,1)S(1)} %all_gather.7), channel_id=1, source_target_pairs={{2,0},{4,2},{6,4},{8,6},{10,8},{12,10},{14,12},{16,14},{18,16},{20... | collective-permute-start | bytes 786440 | tf_op jit(solution)/shard_map/ppermute | solution.py:19
  156.6 20.7 %collective-permute-start.16 = (bf16[128,1024]{1,0:T(8,128)(2,1)S(1)}, bf16[128,1024]{1,0:T(8,128)(2,1)S(1)}, u32[]{:S(2)}, u32[]{:S(2)}) collective-permute-start(bf16[128,1024]{1,0:T(8,128)(2,1)S(1)} %all_gather.7), channel_id=1, source_target_pairs={{4,0},{6,2},{8,4},{10,6},{12,8},{14,10},{16,12},{18,14},{20,16},{2... | collective-permute-start | bytes 786440 | tf_op jit(solution)/shard_map/ppermute | solution.py:19
  166.0 11.4 %collective-permute-start.17 = (bf16[128,1024]{1,0:T(8,128)(2,1)S(1)}, bf16[128,1024]{1,0:T(8,128)(2,1)S(1)}, u32[]{:S(2)}, u32[]{:S(2)}) collective-permute-start(bf16[128,1024]{1,0:T(8,128)(2,1)S(1)} %all_gather.7), channel_id=1, source_target_pairs={{6,0},{8,2},{10,4},{12,6},{14,8},{16,10},{18,12},{20,14},{22,16},{... | collective-permute-start | bytes 786440 | tf_op jit(solution)/shard_map/ppermute | solution.py:19
  217.7 13.5 %collective-permute-start.18 = (bf16[128,1024]{1,0:T(8,128)(2,1)S(1)}, bf16[128,1024]{1,0:T(8,128)(2,1)S(1)}, u32[]{:S(2)}, u32[]{:S(2)}) collective-permute-start(bf16[128,1024]{1,0:T(8,128)(2,1)S(1)} %get-tuple-element.150), channel_id=1, source_target_pairs={{6,0},{8,2},{10,4},{12,6},{14,8},{16,10},{18,12},{20,14},{22,16},{... | collective-permute-start | bytes 786440 | tf_op jit(solution)/shard_map/ppermute | solution.py:19
  225.0 22.0 %collective-permute-start.19 = (bf16[128,1024]{1,0:T(8,128)(2,1)S(1)}, bf16[128,1024]{1,0:T(8,128)(2,1)S(1)}, u32[]{:S(2)}, u32[]{:S(2)}) collective-permute-start(bf16[128,1024]{1,0:T(8,128)(2,1)S(1)} %get-tuple-element.155), channel_id=1, source_target_pairs={{4,0},{6,2},{8,4},{10,6},{12,8},{14,10},{16,12},{18,14},{20,16},{2... | collective-permute-start | bytes 786440 | tf_op jit(solution)/shard_map/ppermute | solution.py:19
  226.4 21.2 %collective-permute-start.20 = (bf16[128,1024]{1,0:T(8,128)(2,1)S(1)}, bf16[128,1024]{1,0:T(8,128)(2,1)S(1)}, u32[]{:S(2)}, u32[]{:S(2)}) collective-permute-start(bf16[128,1024]{1,0:T(8,128)(2,1)S(1)} %get-tuple-element.154), channel_id=1, source_target_pairs={{2,0},{4,2},{6,4},{8,6},{10,8},{12,10},{14,12},{16,14},{18,16},{20... | collective-permute-start | bytes 786440 | tf_op jit(solution)/shard_map/ppermute | solution.py:19
  226.4 21.2 %collective-permute-start.21 = (bf16[128,1024]{1,0:T(8,128)(2,1)S(1)}, bf16[128,1024]{1,0:T(8,128)(2,1)S(1)}, u32[]{:S(2)}, u32[]{:S(2)}) collective-permute-start(bf16[128,1024]{1,0:T(8,128)(2,1)S(1)} %get-tuple-element.153), channel_id=1, source_target_pairs={{254,0},{0,2},{2,4},{4,6},{6,8},{8,10},{10,12},{12,14},{14,16},{16... | collective-permute-start | bytes 786440 | tf_op jit(solution)/shard_map/ppermute | solution.py:19
  228.2 19.5 %collective-permute-start.22 = (bf16[128,1024]{1,0:T(8,128)(2,1)S(1)}, bf16[128,1024]{1,0:T(8,128)(2,1)S(1)}, u32[]{:S(2)}, u32[]{:S(2)}) collective-permute-start(bf16[128,1024]{1,0:T(8,128)(2,1)S(1)} %get-tuple-element.152), channel_id=1, source_target_pairs={{252,0},{254,2},{0,4},{2,6},{4,8},{6,10},{8,12},{10,14},{12,16},{1... | collective-permute-start | bytes 786440 | tf_op jit(solution)/shard_map/ppermute | solution.py:19
  231.2 16.4 %collective-permute-start.23 = (bf16[128,1024]{1,0:T(8,128)(2,1)S(1)}, bf16[128,1024]{1,0:T(8,128)(2,1)S(1)}, u32[]{:S(2)}, u32[]{:S(2)}) collective-permute-start(bf16[128,1024]{1,0:T(8,128)(2,1)S(1)} %get-tuple-element.151), channel_id=1, source_target_pairs={{250,0},{252,2},{254,4},{0,6},{2,8},{4,10},{6,12},{8,14},{10,16},{... | collective-permute-start | bytes 786440 | tf_op jit(solution)/shard_map/ppermute | solution.py:19
Sparse Core Ops, SparseCore 0:
  118.4 19.3 reduce-scatter.2
  249.8 16.8 reduce-scatter.4
where the time goes:
time: 283 us; the launch traced here: 282 us
  waiting for transfers between devices  84.6 us (30%)
  starting transfers between devices  56.9 us (20%)
  matrix products  56.8 us (20%)
  blocking collectives  28.8 us (10%)
  other arithmetic  20.4 us (7%)
  between operations  14.3 us (5%)
  local copies, waits for them, and re-layouts  11.7 us (4%)
  loops' own time  8.08 us (3%)
    ppermute x24, starting transfers between devices, shifted(): return lax.ppermute(block, axis, route)  56.8 us
    ppermute x24, waiting for transfers between devices, shifted(): return lax.ppermute(block, axis, route)  48.6 us
    reduce_scatter x2, waiting for transfers between devices, return_sums(): lax.psum_scatter(collected.astype(jnp.bfloat16), 'grp', scatter_dimension...  35.9 us
    dot_general x6, matrix products, one_group(): lax.dot_general(shares, members, (((0,), (0,)), ((), ())), preferred_elem...  33.4 us
    dot_general x6, matrix products, one_group(): lax.dot_general(members, flat, (((1,), (1,)), ((), ())), preferred_elemen...  23.4 us
    psum x3, blocking collectives, renorm_shard(): totals = lax.psum(squares, 'grp')  16.7 us
    all_gather x2, blocking collectives, fetch_window(): own_block = lax.all_gather(low_copy, 'grp', axis=1, tiled=True)  12.1 us
    another operation x2, loops' own time, score_dense(): partial_value, logs = lax.scan(one_group, start, jnp.arange(groups))  8.08 us
  transfers between devices with their start and end apart: 26, of which 14 were waited for; matrix products, arithmetic and copies ran while one was open for 2% of the time, Pallas kernels for 0%

commit v1 on v0

v1 whole, which is shorter than its diff:
```python
import jax
import jax.numpy as jnp
from jax import lax
from jax.experimental import pallas as pl
from jax.experimental.pallas import tpu as pltpu
from jax.sharding import PartitionSpec as P

D = 1024
HALF = 512
CB = 128
RB = 128
W = 3
ITERS = 2
L = 7
ROWS_LOCAL = 1536
BLOCKS = ROWS_LOCAL // RB
TILE = 256
TILES = ROWS_LOCAL // TILE
CHUNK = 256
CHUNKS = ROWS_LOCAL // CHUNK

EPS = 1e-06
TAU = 20.0
MESH = pl.DeviceIdType.MESH

OWN, PAIR, BACK, AHEAD, FAR, PASS_BACK, PASS_AHEAD = range(7)
COPIES = 13
SCORE_GROUPS = ((OWN, 2), (BACK, 2), (FAR, 1), (PASS_BACK, 2))
SUM_GROUPS = ((PASS_BACK, 2), (BACK, 2), (FAR, 1), (OWN, 2))


def kernel(
    emb,
    cent,
    lists,
    counts,
    out,
    evidence,
    x,
    other_half,
    win,
    weights,
    shares,
    mask,
    total,
    parts,
    arrived,
    pair_sum,
    pair_other,
    full,
    load_sem,
    send_sem,
    recv_sem,
):
    r = lax.axis_index("rows")
    g = lax.axis_index("grp")
    core = r % 2
    pair = r + 1 - 2 * core
    back = (r + 126) % 128
    ahead = (r + 2) % 128
    far = (r + 125 + 6 * core) % 128
    mate = (r, 1 - g)

    def load(i):
        rows = pl.ds(i * CHUNK, CHUNK)
        return pltpu.make_async_copy(emb.at[rows], x.at[rows], load_sem.at[i])

    for i in range(CHUNKS):
        load(i).start()

    barrier = pltpu.get_barrier_semaphore()
    for device in ((pair, g), (back, g), (ahead, g), (far, g), mate):
        pl.semaphore_signal(barrier, inc=1, device_id=device, device_id_type=MESH)
    pl.semaphore_wait(barrier, 5)

    def remote(src, dst, number, device):
        return pltpu.make_async_remote_copy(
            src_ref=src,
            dst_ref=dst,
            send_sem=send_sem.at[number],
            recv_sem=recv_sem.at[number],
            device_id=device,
            device_id_type=MESH,
        )

    first = remote(cent, other_half, ITERS * COPIES, mate)
    first.start()

    slot_places = (
        W,
        W + 1 - 2 * core,
        W - 2,
        W + 2,
        6 * core,
        W - 1 - 2 * core,
        W + 3 - 2 * core,
    )
    ids = lists[...]
    which = lax.broadcasted_iota(jnp.int32, ids.shape, 0)
    nth = lax.broadcasted_iota(jnp.int32, ids.shape, 1)
    lengths = jnp.zeros(ids.shape, jnp.int32)
    for b in range(BLOCKS):
        lengths = jnp.where(which == b, counts[b], lengths)
    places = jnp.where(nth < lengths, (ids + (128 + W) - r) & 127, -1)
    for slot in range(L):
        hit = jnp.max(
            jnp.where(places == slot_places[slot], 1.0, 0.0), axis=1, keepdims=True
        )
        for b in range(BLOCKS):
            mask[slot, :, b * RB : (b + 1) * RB] = jnp.broadcast_to(
                hit[b : b + 1, :], (1, RB)
            )

    for i in range(CHUNKS):
        load(i).wait()

        def normalize(j, carry, i=i):
            rows = pl.ds(pl.multiple_of(i * CHUNK + j * 64, 64), 64)
            v = x[rows, :].astype(jnp.float32)
            m = jnp.mean(v * v, axis=1, keepdims=True)
            x[rows, :] = (v * lax.rsqrt(m + EPS)).astype(jnp.bfloat16)
            return carry

        lax.fori_loop(0, CHUNK // 64, normalize, 0)

    mine = pl.ds(pl.multiple_of(g * HALF, HALF), HALF)
    theirs = pl.ds(pl.multiple_of((1 - g) * HALF, HALF), HALF)
    first.wait()
    a = cent[...]
    b = other_half[...]
    m = (jnp.sum(a * a, axis=1, keepdims=True) + jnp.sum(b * b, axis=1, keepdims=True)) / D
    scale = lax.rsqrt(m + EPS)
    win[0, OWN, :, mine] = (a * scale).astype(jnp.bfloat16)
    win[0, OWN, :, theirs] = (b * scale).astype(jnp.bfloat16)

    for step in range(ITERS):
        base = step * COPIES
        own = win.at[step, OWN]

        fetch = {
            PAIR: remote(own, win.at[step, PAIR], base + 0, (pair, g)),
            AHEAD: remote(own, win.at[step, AHEAD], base + 1, (back, g)),
            BACK: remote(own, win.at[step, BACK], base + 2, (ahead, g)),
            FAR: remote(own, win.at[step, FAR], base + 3, (far, g)),
            PASS_BACK: remote(
                win.at[step, BACK], win.at[step, PASS_BACK], base + 4, (pair, g)
            ),
            PASS_AHEAD: remote(
                win.at[step, AHEAD], win.at[step, PASS_AHEAD], base + 5, (pair, g)
            ),
        }
        for slot in (AHEAD, BACK, FAR, PAIR):
            fetch[slot].start()

        total[...] = jnp.zeros_like(total)
        for start, size in SCORE_GROUPS:
            for slot in range(start, start + size):
                if slot != OWN:
                    fetch[slot].wait_recv()
                if slot == BACK:
                    fetch[PASS_BACK].start()
                if slot == AHEAD:
                    fetch[PASS_AHEAD].start()

            def score(t, carry, start=start, size=size):
                rows = pl.ds(pl.multiple_of(t * TILE, TILE), TILE)
                block = win[step, start : start + size].reshape(size * CB, D)
                s = lax.dot_general(
                    block,
                    x[rows, :],
                    (((1,), (1,)), ((), ())),
                    preferred_element_type=jnp.float32,
                )
                e = jnp.exp(s * (TAU / D))
                added = total[:, rows]
                for k in range(size):
                    w = e[k * CB : (k + 1) * CB, :] * mask[start + k, :, rows]
                    weights[start + k, :, rows] = w
                    added = added + jnp.sum(w, axis=0, keepdims=True)
                total[:, rows] = added
                return carry

            lax.fori_loop(0, TILES, score, 0)

        if step == ITERS - 1:
            evidence[...] = jnp.log(total[...])
        total[...] = 1.0 / total[...]

        returned = {
            PAIR: remote(parts.at[step, PAIR], arrived.at[step, PAIR], base + 6, (pair, g)),
            PASS_BACK: remote(
                parts.at[step, PASS_BACK], arrived.at[step, PASS_BACK], base + 7, (pair, g)
            ),
            PASS_AHEAD: remote(
                parts.at[step, PASS_AHEAD], arrived.at[step, PASS_AHEAD], base + 8, (pair, g)
            ),
            FAR: remote(parts.at[step, FAR], arrived.at[step, FAR], base + 9, (far, g)),
            BACK: remote(parts.at[step, BACK], arrived.at[step, AHEAD], base + 10, (back, g)),
            AHEAD: remote(parts.at[step, AHEAD], arrived.at[step, BACK], base + 11, (ahead, g)),
        }

        for start, size in SUM_GROUPS:

            def share(t, carry, start=start, size=size):
                rows = pl.ds(pl.multiple_of(t * TILE, TILE), TILE)
                inverse = total[:, rows]
                for k in range(size):
                    shares[start * CB + k * CB : start * CB + (k + 1) * CB, rows] = (
                        weights[start + k, :, rows] * inverse
                    ).astype(jnp.bfloat16)
                return carry

            lax.fori_loop(0, TILES, share, 0)
            if start == BACK:
                returned[PASS_BACK].wait_recv()
                returned[PASS_AHEAD].wait_recv()

            def add(t, carry, start=start, size=size):
                columns = pl.ds(pl.multiple_of(t * TILE, TILE), TILE)
                c = jnp.dot(
                    shares[start * CB : (start + size) * CB, :],
                    x[:, columns],
                    preferred_element_type=jnp.float32,
                )
                for k in range(size):
                    slot = start + k
                    piece = c[k * CB : (k + 1) * CB, :]
                    if slot == OWN:
                        full[:, columns] = piece
                        continue
                    if slot in (BACK, AHEAD):
                        passed = PASS_BACK if slot == BACK else PASS_AHEAD
                        piece = piece + arrived[step, passed, :, columns].astype(
                            jnp.float32
                        )
                    parts[step, slot, :, columns] = piece.astype(jnp.bfloat16)
                return carry

            lax.fori_loop(0, D // TILE, add, 0)
            for slot in range(start, start + size):
                if slot != OWN:
                    returned[slot].start()

        for slot in (PAIR, FAR):
            returned[slot].wait_recv()
        returned[BACK].wait_recv()
        returned[AHEAD].wait_recv()

        for j in range(CB // 32):
            rows = slice(j * 32, (j + 1) * 32)
            v = full[rows, :]
            for slot in (PAIR, FAR, BACK, AHEAD):
                v = v + arrived[step, slot, rows, :].astype(jnp.float32)
            pair_sum[step, rows, :] = v.astype(jnp.bfloat16)
        swap = remote(pair_sum.at[step], pair_other.at[step], base + 12, mate)
        swap.start()
        swap.wait_recv()
        for j in range(CB // 32):
            rows = slice(j * 32, (j + 1) * 32)
            v = pair_sum[step, rows, :].astype(jnp.float32) + pair_other[
                step, rows, :
            ].astype(jnp.float32)
            m = jnp.mean(v * v, axis=1, keepdims=True)
            v = v * lax.rsqrt(m + EPS)
            if step < ITERS - 1:
                win[step + 1, OWN, rows, :] = v.astype(jnp.bfloat16)
            else:
                full[rows, :] = v
        if step == ITERS - 1:
            out[...] = full[:, mine]

        for copy in list(fetch.values()) + list(returned.values()) + [swap]:
            copy.wait_send()


def local(embeddings, centroids, block_lists, block_counts):
    vmem = pl.BlockSpec(memory_space=pltpu.VMEM)
    copies = ITERS * COPIES + 1
    current, evidence = pl.pallas_call(
        kernel,
        out_shape=(
            jax.ShapeDtypeStruct((CB, HALF), jnp.float32),
            jax.ShapeDtypeStruct((1, ROWS_LOCAL), jnp.float32),
        ),
        in_specs=[
            pl.BlockSpec(memory_space=pl.ANY),
            vmem,
            vmem,
            pl.BlockSpec(memory_space=pltpu.SMEM),
        ],
        out_specs=(vmem, vmem),
        scratch_shapes=[
            pltpu.VMEM((ROWS_LOCAL, D), jnp.bfloat16),
            pltpu.VMEM((CB, HALF), jnp.float32),
            pltpu.VMEM((ITERS, L, CB, D), jnp.bfloat16),
            pltpu.VMEM((L, CB, ROWS_LOCAL), jnp.float32),
            pltpu.VMEM((L * CB, ROWS_LOCAL), jnp.bfloat16),
            pltpu.VMEM((L, 1, ROWS_LOCAL), jnp.float32),
            pltpu.VMEM((1, ROWS_LOCAL), jnp.float32),
            pltpu.VMEM((ITERS, L, CB, D), jnp.bfloat16),
            pltpu.VMEM((ITERS, L, CB, D), jnp.bfloat16),
            pltpu.VMEM((ITERS, CB, D), jnp.bfloat16),
            pltpu.VMEM((ITERS, CB, D), jnp.bfloat16),
            pltpu.VMEM((CB, D), jnp.float32),
            pltpu.SemaphoreType.DMA((CHUNKS,)),
            pltpu.SemaphoreType.DMA((copies,)),
            pltpu.SemaphoreType.DMA((copies,)),
        ],
        compiler_params=pltpu.CompilerParams(
            collective_id=0, has_side_effects=True, vmem_limit_bytes=60 * 1024 * 1024
        ),
        name="kmeans",
    )(embeddings, centroids, block_lists, block_counts)
    return (current, evidence.reshape(ROWS_LOCAL))


def solution(mesh):
    return jax.shard_map(
        local,
        mesh=mesh,
        in_specs=(
            P(("rows", "grp"), None),
            P("rows", "grp"),
            P(("rows", "grp"), None),
            P(("rows", "grp")),
        ),
        out_specs=(P("rows", "grp"), P(("rows", "grp"))),
        check_vma=False,
    )
```

time: 283 us -> 116 us (0.41)
  Pallas kernels: 0 us -> 111 us
  waiting for transfers between devices: 84.6 us -> 0 us
  starting transfers between devices: 56.9 us -> 0 us
  matrix products: 56.8 us -> 0 us
  blocking collectives: 28.8 us -> 0 us
  other arithmetic: 20.4 us -> 1.31 us
  between operations: 14.3 us -> 0.64 us
  local copies, waits for them, and re-layouts: 11.7 us -> 3.04 us
  loops' own time: 8.08 us -> 0 us
    pallas_call x0 -> x1, Pallas kernels: none -> 111 us  [local(): pl.pallas_call(kernel, out_shape=(jax.ShapeDtypeStruct((CB, HALF), jnp.fl...]
    dot_general x12 -> x0, matrix products: 56.8 us -> none  [the longest x6 33.4 us: one_group(): lax.dot_general(shares, members, (((0,), (0,)), ((), ())), preferred_elem...]
    ppermute x24 -> x0, starting transfers between devices: 56.8 us -> none  [shifted(): return lax.ppermute(block, axis, route)]
    ppermute x24 -> x0, waiting for transfers between devices: 48.6 us -> none  [shifted(): return lax.ppermute(block, axis, route)]
    reduce_scatter x2 -> x0, waiting for transfers between devices: 35.9 us -> none  [return_sums(): lax.psum_scatter(collected.astype(jnp.bfloat16), 'grp', scatter_dimension...]
    psum x3 -> x0, blocking collectives: 16.7 us -> none  [renorm_shard(): totals = lax.psum(squares, 'grp')]
    all_gather x2 -> x0, blocking collectives: 12.1 us -> none  [fetch_window(): own_block = lax.all_gather(low_copy, 'grp', axis=1, tiled=True)]
    convert_element_type x5 -> x0, other arithmetic: 8.33 us -> none  [the longest x2 4.04 us: return_sums(): collected.astype(jnp.bfloat16)]
  transfers between devices with their start and end apart: 26 -> 0, of which waited for: 14 -> 0; matrix products, arithmetic and copies ran while one was open for 2% -> 0% of each run, Pallas kernels for 0% -> 0%
where the time goes in v1:
time: 116 us
  Pallas kernels  111 us (96%)
  local copies, waits for them, and re-layouts  3.04 us (3%)
  other arithmetic  1.31 us (1%)
    pallas_call x1, Pallas kernels, local(): pl.pallas_call(kernel, out_shape=(jax.ShapeDtypeStruct((CB, HALF), jnp.fl...  111 us
    unnamed x2, local copies, waits for them, and re-layouts  3.04 us

profile of v1, /device:TPU:1, one launch (start us, length us, event | category | flops | bytes accessed | tf_op | source)
XLA Modules:
  0.0 116.1 jit_solution(5135628480803541580)
XLA Ops:
  0.6 1.4 %copy.6.lists = s32[12,7]{1,0:T(8,128)} copy(s32[12,7]{0,1:T(8,128)} %param.6) | data formatting | bytes 672 | tf_op args[2]
  2.0 111.2 %kmeans.1 = (f32[128,512]{1,0:T(8,128)}, f32[1,1536]{1,0:T(1,128)}) custom-call(bf16[1536,1024]{1,0:T(8,128)(2,1)} %emb.1, f32[128,512]{1,0:T(8,128)} %cent.1, s32[12,7]{1,0:T(8,128)} %copy.6.lists, s32[12]{0:T(128)} %counts.1), custom_call_target="tpu_custom_call" | custom-call | tf_op jit(solution)/shard_map/kmeans/pallas_call | solution.py:279
  113.2 1.3 %reduce = f32[1536]{0:T(1024)} reduce(f32[1,1536]{1,0:T(1,128)} %get-tuple-element.5, f32[]{:T(128)} %constant.2), dimensions={0}, to_apply=%get-tuple-element.5.reduce_sub_computation | reduce | bytes 12292 | tf_op jit(solution)/shard_map/kmeans/pallas_call | solution.py:279
  114.5 1.7 %copy.8 = f32[128,512]{1,0:T(8,128)} copy(f32[128,512]{1,0:T(8,128)} %get-tuple-element.8) | data formatting | bytes 524288

commit v2 on v1

--- a/solution.py
+++ b/solution.py
@@ -14,8 +14,10 @@
 L = 7
 ROWS_LOCAL = 1536
 BLOCKS = ROWS_LOCAL // RB
-TILE = 256
+TILE = 512
 TILES = ROWS_LOCAL // TILE
+PIECES = 4
+PIECE = CB // PIECES
 CHUNK = 256
 CHUNKS = ROWS_LOCAL // CHUNK
 
@@ -24,7 +26,7 @@
 MESH = pl.DeviceIdType.MESH
 
 OWN, PAIR, BACK, AHEAD, FAR, PASS_BACK, PASS_AHEAD = range(7)
-COPIES = 13
+COPIES = 12
 SCORE_GROUPS = ((OWN, 2), (BACK, 2), (FAR, 1), (PASS_BACK, 2))
 SUM_GROUPS = ((PASS_BACK, 2), (BACK, 2), (FAR, 1), (OWN, 2))
 
@@ -37,6 +39,7 @@
     out,
     evidence,
     x,
+    xt,
     other_half,
     win,
     weights,
@@ -48,9 +51,13 @@
     pair_sum,
     pair_other,
     full,
+    hop_first,
+    hop,
     load_sem,
     send_sem,
     recv_sem,
+    swap_send_sem,
+    swap_recv_sem,
 ):
     r = lax.axis_index("rows")
     g = lax.axis_index("grp")
@@ -59,7 +66,9 @@
     back = (r + 126) % 128
     ahead = (r + 2) % 128
     far = (r + 125 + 6 * core) % 128
-    mate = (r, 1 - g)
+    beside = r + 2 - 4 * (r % 4 // 2)
+    same_side = (beside, g)
+    other_side = (beside, 1 - g)
 
     def load(i):
         rows = pl.ds(i * CHUNK, CHUNK)
@@ -69,7 +78,7 @@
         load(i).start()
 
     barrier = pltpu.get_barrier_semaphore()
-    for device in ((pair, g), (back, g), (ahead, g), (far, g), mate):
+    for device in ((pair, g), (back, g), (ahead, g), (far, g), other_side):
         pl.semaphore_signal(barrier, inc=1, device_id=device, device_id_type=MESH)
     pl.semaphore_wait(barrier, 5)
 
@@ -83,8 +92,29 @@
             device_id_type=MESH,
         )
 
-    first = remote(cent, other_half, ITERS * COPIES, mate)
-    first.start()
+    def swap_copy(src, dst, number, device):
+        return pltpu.make_async_remote_copy(
+            src_ref=src,
+            dst_ref=dst,
+            send_sem=swap_send_sem.at[number],
+            recv_sem=swap_recv_sem.at[number],
+            device_id=device,
+            device_id_type=MESH,
+        )
+
+    def swap(src, middle, dst, turn):
+        out_hops, in_hops = [], []
+        for j in range(PIECES):
+            rows = pl.ds(j * PIECE, PIECE)
+            number = (turn * PIECES + j) * 2
+            ways = (same_side, other_side) if j % 2 == 0 else (other_side, same_side)
+            out_hops.append(swap_copy(src.at[rows], middle.at[rows], number, ways[0]))
+            in_hops.append(swap_copy(middle.at[rows], dst.at[rows], number + 1, ways[1]))
+        return out_hops, in_hops
+
+    first_out, first_in = swap(cent, hop_first, other_half, ITERS)
+    for copy in first_out:
+        copy.start()
 
     slot_places = (
         W,
@@ -111,21 +141,28 @@
                 hit[b : b + 1, :], (1, RB)
             )
 
+    for j in range(PIECES):
+        first_out[j].wait_recv()
+        first_in[j].start()
+
     for i in range(CHUNKS):
         load(i).wait()
 
         def normalize(j, carry, i=i):
-            rows = pl.ds(pl.multiple_of(i * CHUNK + j * 64, 64), 64)
+            rows = pl.ds(pl.multiple_of(i * CHUNK + j * 128, 128), 128)
             v = x[rows, :].astype(jnp.float32)
             m = jnp.mean(v * v, axis=1, keepdims=True)
-            x[rows, :] = (v * lax.rsqrt(m + EPS)).astype(jnp.bfloat16)
+            y = (v * lax.rsqrt(m + EPS)).astype(jnp.bfloat16)
+            x[rows, :] = y
+            xt[:, rows] = y.T
             return carry
 
-        lax.fori_loop(0, CHUNK // 64, normalize, 0)
+        lax.fori_loop(0, CHUNK // 128, normalize, 0)
 
     mine = pl.ds(pl.multiple_of(g * HALF, HALF), HALF)
     theirs = pl.ds(pl.multiple_of((1 - g) * HALF, HALF), HALF)
-    first.wait()
+    for copy in first_in:
+        copy.wait_recv()
     a = cent[...]
     b = other_half[...]
     m = (jnp.sum(a * a, axis=1, keepdims=True) + jnp.sum(b * b, axis=1, keepdims=True)) / D
@@ -167,8 +204,8 @@
                 block = win[step, start : start + size].reshape(size * CB, D)
                 s = lax.dot_general(
                     block,
-                    x[rows, :],
-                    (((1,), (1,)), ((), ())),
+                    xt[:, rows],
+                    (((1,), (0,)), ((), ())),
                     preferred_element_type=jnp.float32,
                 )
                 e = jnp.exp(s * (TAU / D))
@@ -246,17 +283,22 @@
         returned[BACK].wait_recv()
         returned[AHEAD].wait_recv()
 
-        for j in range(CB // 32):
-            rows = slice(j * 32, (j + 1) * 32)
+        swap_out, swap_in = swap(
+            pair_sum.at[step], hop.at[step], pair_other.at[step], step
+        )
+        for j in range(PIECES):
+            rows = slice(j * PIECE, (j + 1) * PIECE)
             v = full[rows, :]
             for slot in (PAIR, FAR, BACK, AHEAD):
                 v = v + arrived[step, slot, rows, :].astype(jnp.float32)
             pair_sum[step, rows, :] = v.astype(jnp.bfloat16)
-        swap = remote(pair_sum.at[step], pair_other.at[step], base + 12, mate)
-        swap.start()
-        swap.wait_recv()
-        for j in range(CB // 32):
-            rows = slice(j * 32, (j + 1) * 32)
+            swap_out[j].start()
+        for j in range(PIECES):
+            swap_out[j].wait_recv()
+            swap_in[j].start()
+        for j in range(PIECES):
+            rows = slice(j * PIECE, (j + 1) * PIECE)
+            swap_in[j].wait_recv()
             v = pair_sum[step, rows, :].astype(jnp.float32) + pair_other[
                 step, rows, :
             ].astype(jnp.float32)
@@ -269,13 +311,17 @@
         if step == ITERS - 1:
             out[...] = full[:, mine]
 
-        for copy in list(fetch.values()) + list(returned.values()) + [swap]:
+        for copy in list(fetch.values()) + list(returned.values()) + swap_out + swap_in:
             copy.wait_send()
+
+    for copy in first_out + first_in:
+        copy.wait_send()
 
 
 def local(embeddings, centroids, block_lists, block_counts):
     vmem = pl.BlockSpec(memory_space=pltpu.VMEM)
-    copies = ITERS * COPIES + 1
+    copies = ITERS * COPIES
+    swaps = (ITERS + 1) * PIECES * 2
     current, evidence = pl.pallas_call(
         kernel,
         out_shape=(
@@ -291,6 +337,7 @@
         out_specs=(vmem, vmem),
         scratch_shapes=[
             pltpu.VMEM((ROWS_LOCAL, D), jnp.bfloat16),
+            pltpu.VMEM((D, ROWS_LOCAL), jnp.bfloat16),
             pltpu.VMEM((CB, HALF), jnp.float32),
             pltpu.VMEM((ITERS, L, CB, D), jnp.bfloat16),
             pltpu.VMEM((L, CB, ROWS_LOCAL), jnp.float32),
@@ -302,9 +349,13 @@
             pltpu.VMEM((ITERS, CB, D), jnp.bfloat16),
             pltpu.VMEM((ITERS, CB, D), jnp.bfloat16),
             pltpu.VMEM((CB, D), jnp.float32),
+            pltpu.VMEM((CB, HALF), jnp.float32),
+            pltpu.VMEM((ITERS, CB, D), jnp.bfloat16),
             pltpu.SemaphoreType.DMA((CHUNKS,)),
             pltpu.SemaphoreType.DMA((copies,)),
             pltpu.SemaphoreType.DMA((copies,)),
+            pltpu.SemaphoreType.DMA((swaps,)),
+            pltpu.SemaphoreType.DMA((swaps,)),
         ],
         compiler_params=pltpu.CompilerParams(
             collective_id=0, has_side_effects=True, vmem_limit_bytes=60 * 1024 * 1024

time: 116 us -> 111 us (0.957); the launches traced: 116 us -> 110 us
  Pallas kernels: 111 us -> 105 us
    pallas_call x1, Pallas kernels: 111 us -> 105 us  [local(): pl.pallas_call(kernel, out_shape=(jax.ShapeDtypeStruct((CB, HALF), jnp.fl...]
where the time goes in v2:
time: 111 us; the launch traced here: 110 us
  Pallas kernels  105 us (95%)
  local copies, waits for them, and re-layouts  3.04 us (3%)
  other arithmetic  1.31 us (1%)
    pallas_call x1, Pallas kernels, local(): pl.pallas_call(kernel, out_shape=(jax.ShapeDtypeStruct((CB, HALF), jnp.fl...  105 us
    unnamed x2, local copies, waits for them, and re-layouts  3.04 us

profile of v2, /device:TPU:1, one launch (start us, length us, event | category | flops | bytes accessed | tf_op | source)
XLA Modules:
  0.0 109.8 jit_solution(11994787390078297929)
XLA Ops:
  0.6 1.4 %copy.6.lists = s32[12,7]{1,0:T(8,128)} copy(s32[12,7]{0,1:T(8,128)} %param.6) | data formatting | bytes 672 | tf_op args[2]
  2.0 104.8 %kmeans.1 = (f32[128,512]{1,0:T(8,128)}, f32[1,1536]{1,0:T(1,128)}) custom-call(bf16[1536,1024]{1,0:T(8,128)(2,1)} %emb.1, f32[128,512]{1,0:T(8,128)} %cent.1, s32[12,7]{1,0:T(8,128)} %copy.6.lists, s32[12]{0:T(128)} %counts.1), custom_call_target="tpu_custom_call" | custom-call | tf_op jit(solution)/shard_map/kmeans/pallas_call | solution.py:325
  106.8 1.3 %reduce = f32[1536]{0:T(1024)} reduce(f32[1,1536]{1,0:T(1,128)} %get-tuple-element.5, f32[]{:T(128)} %constant.2), dimensions={0}, to_apply=%get-tuple-element.5.reduce_sub_computation | reduce | bytes 12292 | tf_op jit(solution)/shard_map/kmeans/pallas_call | solution.py:325
  108.1 1.7 %copy.8 = f32[128,512]{1,0:T(8,128)} copy(f32[128,512]{1,0:T(8,128)} %get-tuple-element.8) | data formatting | bytes 524288

commit v3 on v2

--- a/solution.py
+++ b/solution.py
@@ -14,8 +14,9 @@
 L = 7
 ROWS_LOCAL = 1536
 BLOCKS = ROWS_LOCAL // RB
-TILE = 512
+TILE = 768
 TILES = ROWS_LOCAL // TILE
+COLUMNS = 1024
 PIECES = 4
 PIECE = CB // PIECES
 CHUNK = 256
@@ -27,7 +28,7 @@
 
 OWN, PAIR, BACK, AHEAD, FAR, PASS_BACK, PASS_AHEAD = range(7)
 COPIES = 12
-SCORE_GROUPS = ((OWN, 2), (BACK, 2), (FAR, 1), (PASS_BACK, 2))
+SCORE_GROUPS = ((OWN, 2), (FAR, 1), (BACK, 2), (PASS_BACK, 2))
 SUM_GROUPS = ((PASS_BACK, 2), (BACK, 2), (FAR, 1), (OWN, 2))
 
 
@@ -51,8 +52,6 @@
     pair_sum,
     pair_other,
     full,
-    hop_first,
-    hop,
     load_sem,
     send_sem,
     recv_sem,
@@ -66,9 +65,10 @@
     back = (r + 126) % 128
     ahead = (r + 2) % 128
     far = (r + 125 + 6 * core) % 128
-    beside = r + 2 - 4 * (r % 4 // 2)
-    same_side = (beside, g)
-    other_side = (beside, 1 - g)
+    mate = (r, 1 - g)
+    low = r % 4 // 2
+    back_at = (back, (g + 1 - low) % 2)
+    ahead_at = (ahead, (g + low) % 2)
 
     def load(i):
         rows = pl.ds(i * CHUNK, CHUNK)
@@ -78,7 +78,7 @@
         load(i).start()
 
     barrier = pltpu.get_barrier_semaphore()
-    for device in ((pair, g), (back, g), (ahead, g), (far, g), other_side):
+    for device in ((pair, g), back_at, ahead_at, (far, g), mate):
         pl.semaphore_signal(barrier, inc=1, device_id=device, device_id_type=MESH)
     pl.semaphore_wait(barrier, 5)
 
@@ -102,18 +102,19 @@
             device_id_type=MESH,
         )
 
-    def swap(src, middle, dst, turn):
-        out_hops, in_hops = [], []
-        for j in range(PIECES):
-            rows = pl.ds(j * PIECE, PIECE)
-            number = (turn * PIECES + j) * 2
-            ways = (same_side, other_side) if j % 2 == 0 else (other_side, same_side)
-            out_hops.append(swap_copy(src.at[rows], middle.at[rows], number, ways[0]))
-            in_hops.append(swap_copy(middle.at[rows], dst.at[rows], number + 1, ways[1]))
-        return out_hops, in_hops
-
-    first_out, first_in = swap(cent, hop_first, other_half, ITERS)
-    for copy in first_out:
+    def swap(src, dst, turn):
+        return [
+            swap_copy(
+                src.at[pl.ds(j * PIECE, PIECE)],
+                dst.at[pl.ds(j * PIECE, PIECE)],
+                turn * PIECES + j,
+                mate,
+            )
+            for j in range(PIECES)
+        ]
+
+    first = swap(cent, other_half, ITERS)
+    for copy in first:
         copy.start()
 
     slot_places = (
@@ -141,10 +142,6 @@
                 hit[b : b + 1, :], (1, RB)
             )
 
-    for j in range(PIECES):
-        first_out[j].wait_recv()
-        first_in[j].start()
-
     for i in range(CHUNKS):
         load(i).wait()
 
@@ -161,7 +158,7 @@
 
     mine = pl.ds(pl.multiple_of(g * HALF, HALF), HALF)
     theirs = pl.ds(pl.multiple_of((1 - g) * HALF, HALF), HALF)
-    for copy in first_in:
+    for copy in first:
         copy.wait_recv()
     a = cent[...]
     b = other_half[...]
@@ -176,8 +173,8 @@
 
         fetch = {
             PAIR: remote(own, win.at[step, PAIR], base + 0, (pair, g)),
-            AHEAD: remote(own, win.at[step, AHEAD], base + 1, (back, g)),
-            BACK: remote(own, win.at[step, BACK], base + 2, (ahead, g)),
+            AHEAD: remote(own, win.at[step, AHEAD], base + 1, back_at),
+            BACK: remote(own, win.at[step, BACK], base + 2, ahead_at),
             FAR: remote(own, win.at[step, FAR], base + 3, (far, g)),
             PASS_BACK: remote(
                 win.at[step, BACK], win.at[step, PASS_BACK], base + 4, (pair, g)
@@ -232,8 +229,8 @@
                 parts.at[step, PASS_AHEAD], arrived.at[step, PASS_AHEAD], base + 8, (pair, g)
             ),
             FAR: remote(parts.at[step, FAR], arrived.at[step, FAR], base + 9, (far, g)),
-            BACK: remote(parts.at[step, BACK], arrived.at[step, AHEAD], base + 10, (back, g)),
-            AHEAD: remote(parts.at[step, AHEAD], arrived.at[step, BACK], base + 11, (ahead, g)),
+            BACK: remote(parts.at[step, BACK], arrived.at[step, AHEAD], base + 10, back_at),
+            AHEAD: remote(parts.at[step, AHEAD], arrived.at[step, BACK], base + 11, ahead_at),
         }
 
         for start, size in SUM_GROUPS:
@@ -253,7 +250,7 @@
                 returned[PASS_AHEAD].wait_recv()
 
             def add(t, carry, start=start, size=size):
-                columns = pl.ds(pl.multiple_of(t * TILE, TILE), TILE)
+                columns = pl.ds(pl.multiple_of(t * COLUMNS, COLUMNS), COLUMNS)
                 c = jnp.dot(
                     shares[start * CB : (start + size) * CB, :],
                     x[:, columns],
@@ -273,7 +270,7 @@
                     parts[step, slot, :, columns] = piece.astype(jnp.bfloat16)
                 return carry
 
-            lax.fori_loop(0, D // TILE, add, 0)
+            lax.fori_loop(0, D // COLUMNS, add, 0)
             for slot in range(start, start + size):
                 if slot != OWN:
                     returned[slot].start()
@@ -283,22 +280,17 @@
         returned[BACK].wait_recv()
         returned[AHEAD].wait_recv()
 
-        swap_out, swap_in = swap(
-            pair_sum.at[step], hop.at[step], pair_other.at[step], step
-        )
+        swaps = swap(pair_sum.at[step], pair_other.at[step], step)
         for j in range(PIECES):
             rows = slice(j * PIECE, (j + 1) * PIECE)
             v = full[rows, :]
             for slot in (PAIR, FAR, BACK, AHEAD):
                 v = v + arrived[step, slot, rows, :].astype(jnp.float32)
             pair_sum[step, rows, :] = v.astype(jnp.bfloat16)
-            swap_out[j].start()
-        for j in range(PIECES):
-            swap_out[j].wait_recv()
-            swap_in[j].start()
+            swaps[j].start()
         for j in range(PIECES):
             rows = slice(j * PIECE, (j + 1) * PIECE)
-            swap_in[j].wait_recv()
+            swaps[j].wait_recv()
             v = pair_sum[step, rows, :].astype(jnp.float32) + pair_other[
                 step, rows, :
             ].astype(jnp.float32)
@@ -311,17 +303,17 @@
         if step == ITERS - 1:
             out[...] = full[:, mine]
 
-        for copy in list(fetch.values()) + list(returned.values()) + swap_out + swap_in:
+        for copy in list(fetch.values()) + list(returned.values()) + swaps:
             copy.wait_send()
 
-    for copy in first_out + first_in:
+    for copy in first:
         copy.wait_send()
 
 
 def local(embeddings, centroids, block_lists, block_counts):
     vmem = pl.BlockSpec(memory_space=pltpu.VMEM)
     copies = ITERS * COPIES
-    swaps = (ITERS + 1) * PIECES * 2
+    swaps = (ITERS + 1) * PIECES
     current, evidence = pl.pallas_call(
         kernel,
         out_shape=(
@@ -349,8 +341,6 @@
             pltpu.VMEM((ITERS, CB, D), jnp.bfloat16),
             pltpu.VMEM((ITERS, CB, D), jnp.bfloat16),
             pltpu.VMEM((CB, D), jnp.float32),
-            pltpu.VMEM((CB, HALF), jnp.float32),
-            pltpu.VMEM((ITERS, CB, D), jnp.bfloat16),
             pltpu.SemaphoreType.DMA((CHUNKS,)),
             pltpu.SemaphoreType.DMA((copies,)),
             pltpu.SemaphoreType.DMA((copies,)),

time: 111 us -> 95.1 us (0.86)
  Pallas kernels: 105 us -> 88.5 us
    pallas_call x1, Pallas kernels: 105 us -> 88.5 us  [local(): pl.pallas_call(kernel, out_shape=(jax.ShapeDtypeStruct((CB, HALF), jnp.fl...]
where the time goes in v3:
time: 95.1 us; the launch traced here: 93.5 us
  Pallas kernels  88.5 us (93%)
  local copies, waits for them, and re-layouts  3.04 us (3%)
  other arithmetic  1.31 us (1%)
    pallas_call x1, Pallas kernels, local(): pl.pallas_call(kernel, out_shape=(jax.ShapeDtypeStruct((CB, HALF), jnp.fl...  88.5 us
    unnamed x2, local copies, waits for them, and re-layouts  3.04 us

profile of v3, /device:TPU:1, one launch (start us, length us, event | category | flops | bytes accessed | tf_op | source)
XLA Modules:
  0.0 93.5 jit_solution(7237077961704806784)
XLA Ops:
  0.6 1.4 %copy.6.lists = s32[12,7]{1,0:T(8,128)} copy(s32[12,7]{0,1:T(8,128)} %param.6) | data formatting | bytes 672 | tf_op args[2]
  2.0 88.5 %kmeans.1 = (f32[128,512]{1,0:T(8,128)}, f32[1,1536]{1,0:T(1,128)}) custom-call(bf16[1536,1024]{1,0:T(8,128)(2,1)} %emb.1, f32[128,512]{1,0:T(8,128)} %cent.1, s32[12,7]{1,0:T(8,128)} %copy.6.lists, s32[12]{0:T(128)} %counts.1), custom_call_target="tpu_custom_call" | custom-call | tf_op jit(solution)/shard_map/kmeans/pallas_call | solution.py:317
  90.5 1.3 %reduce = f32[1536]{0:T(1024)} reduce(f32[1,1536]{1,0:T(1,128)} %get-tuple-element.5, f32[]{:T(128)} %constant.2), dimensions={0}, to_apply=%get-tuple-element.5.reduce_sub_computation | reduce | bytes 12292 | tf_op jit(solution)/shard_map/kmeans/pallas_call | solution.py:317
  91.8 1.7 %copy.8 = f32[128,512]{1,0:T(8,128)} copy(f32[128,512]{1,0:T(8,128)} %get-tuple-element.8) | data formatting | bytes 524288

commit v4 on v3

--- a/solution.py
+++ b/solution.py
@@ -19,6 +19,7 @@
 COLUMNS = 1024
 PIECES = 4
 PIECE = CB // PIECES
+SPAN = CB // 2
 CHUNK = 256
 CHUNKS = ROWS_LOCAL // CHUNK
 
@@ -28,7 +29,7 @@
 
 OWN, PAIR, BACK, AHEAD, FAR, PASS_BACK, PASS_AHEAD = range(7)
 COPIES = 12
-SCORE_GROUPS = ((OWN, 2), (FAR, 1), (BACK, 2), (PASS_BACK, 2))
+SCORE_GROUPS = ((OWN, 2), (BACK, 2), (FAR, 1), (PASS_BACK, 2))
 SUM_GROUPS = ((PASS_BACK, 2), (BACK, 2), (FAR, 1), (OWN, 2))
 
 
@@ -167,34 +168,53 @@
     win[0, OWN, :, mine] = (a * scale).astype(jnp.bfloat16)
     win[0, OWN, :, theirs] = (b * scale).astype(jnp.bfloat16)
 
+    def halves(src, dst, number, device):
+        return [
+            remote(
+                src.at[pl.ds(h * SPAN, SPAN)],
+                dst.at[pl.ds(h * SPAN, SPAN)],
+                number * 2 + h,
+                device,
+            )
+            for h in range(2)
+        ]
+
+    fetches = []
     for step in range(ITERS):
         base = step * COPIES
-        own = win.at[step, OWN]
-
-        fetch = {
-            PAIR: remote(own, win.at[step, PAIR], base + 0, (pair, g)),
-            AHEAD: remote(own, win.at[step, AHEAD], base + 1, back_at),
-            BACK: remote(own, win.at[step, BACK], base + 2, ahead_at),
-            FAR: remote(own, win.at[step, FAR], base + 3, (far, g)),
-            PASS_BACK: remote(
-                win.at[step, BACK], win.at[step, PASS_BACK], base + 4, (pair, g)
-            ),
-            PASS_AHEAD: remote(
-                win.at[step, AHEAD], win.at[step, PASS_AHEAD], base + 5, (pair, g)
-            ),
-        }
+        slots = [win.at[step, slot] for slot in range(L)]
+        fetches.append(
+            {
+                PAIR: halves(slots[OWN], slots[PAIR], base + 0, (pair, g)),
+                AHEAD: halves(slots[OWN], slots[AHEAD], base + 1, back_at),
+                BACK: halves(slots[OWN], slots[BACK], base + 2, ahead_at),
+                FAR: halves(slots[OWN], slots[FAR], base + 3, (far, g)),
+                PASS_BACK: halves(slots[BACK], slots[PASS_BACK], base + 4, (pair, g)),
+                PASS_AHEAD: halves(slots[AHEAD], slots[PASS_AHEAD], base + 5, (pair, g)),
+            }
+        )
+
+    def start_fetch(step, h):
         for slot in (AHEAD, BACK, FAR, PAIR):
-            fetch[slot].start()
+            fetches[step][slot][h].start()
+
+    for h in range(2):
+        start_fetch(0, h)
+
+    for step in range(ITERS):
+        base = step * COPIES
+        fetch = fetches[step]
 
         total[...] = jnp.zeros_like(total)
         for start, size in SCORE_GROUPS:
             for slot in range(start, start + size):
-                if slot != OWN:
-                    fetch[slot].wait_recv()
-                if slot == BACK:
-                    fetch[PASS_BACK].start()
-                if slot == AHEAD:
-                    fetch[PASS_AHEAD].start()
+                for h in range(2):
+                    if slot != OWN:
+                        fetch[slot][h].wait_recv()
+                    if slot == BACK:
+                        fetch[PASS_BACK][h].start()
+                    if slot == AHEAD:
+                        fetch[PASS_AHEAD][h].start()
 
             def score(t, carry, start=start, size=size):
                 rows = pl.ds(pl.multiple_of(t * TILE, TILE), TILE)
@@ -221,16 +241,16 @@
         total[...] = 1.0 / total[...]
 
         returned = {
-            PAIR: remote(parts.at[step, PAIR], arrived.at[step, PAIR], base + 6, (pair, g)),
-            PASS_BACK: remote(
+            PAIR: halves(parts.at[step, PAIR], arrived.at[step, PAIR], base + 6, (pair, g)),
+            PASS_BACK: halves(
                 parts.at[step, PASS_BACK], arrived.at[step, PASS_BACK], base + 7, (pair, g)
             ),
-            PASS_AHEAD: remote(
+            PASS_AHEAD: halves(
                 parts.at[step, PASS_AHEAD], arrived.at[step, PASS_AHEAD], base + 8, (pair, g)
             ),
-            FAR: remote(parts.at[step, FAR], arrived.at[step, FAR], base + 9, (far, g)),
-            BACK: remote(parts.at[step, BACK], arrived.at[step, AHEAD], base + 10, back_at),
-            AHEAD: remote(parts.at[step, AHEAD], arrived.at[step, BACK], base + 11, ahead_at),
+            FAR: halves(parts.at[step, FAR], arrived.at[step, FAR], base + 9, (far, g)),
+            BACK: halves(parts.at[step, BACK], arrived.at[step, AHEAD], base + 10, back_at),
+            AHEAD: halves(parts.at[step, AHEAD], arrived.at[step, BACK], base + 11, ahead_at),
         }
 
         for start, size in SUM_GROUPS:
@@ -246,8 +266,9 @@
 
             lax.fori_loop(0, TILES, share, 0)
             if start == BACK:
-                returned[PASS_BACK].wait_recv()
-                returned[PASS_AHEAD].wait_recv()
+                for h in range(2):
+                    returned[PASS_BACK][h].wait_recv()
+                    returned[PASS_AHEAD][h].wait_recv()
 
             def add(t, carry, start=start, size=size):
                 columns = pl.ds(pl.multiple_of(t * COLUMNS, COLUMNS), COLUMNS)
@@ -273,16 +294,15 @@
             lax.fori_loop(0, D // COLUMNS, add, 0)
             for slot in range(start, start + size):
                 if slot != OWN:
-                    returned[slot].start()
-
-        for slot in (PAIR, FAR):
-            returned[slot].wait_recv()
-        returned[BACK].wait_recv()
-        returned[AHEAD].wait_recv()
+                    for h in range(2):
+                        returned[slot][h].start()
 
         swaps = swap(pair_sum.at[step], pair_other.at[step], step)
         for j in range(PIECES):
             rows = slice(j * PIECE, (j + 1) * PIECE)
+            if j * 2 % PIECES == 0:
+                for slot in (PAIR, FAR, BACK, AHEAD):
+                    returned[slot][j * 2 // PIECES].wait_recv()
             v = full[rows, :]
             for slot in (PAIR, FAR, BACK, AHEAD):
                 v = v + arrived[step, slot, rows, :].astype(jnp.float32)
@@ -298,13 +318,16 @@
             v = v * lax.rsqrt(m + EPS)
             if step < ITERS - 1:
                 win[step + 1, OWN, rows, :] = v.astype(jnp.bfloat16)
+                if (j + 1) * 2 % PIECES == 0:
+                    start_fetch(step + 1, (j + 1) * 2 // PIECES - 1)
             else:
                 full[rows, :] = v
         if step == ITERS - 1:
             out[...] = full[:, mine]
 
-        for copy in list(fetch.values()) + list(returned.values()) + swaps:
-            copy.wait_send()
+        for copies in list(fetch.values()) + list(returned.values()) + [swaps]:
+            for copy in copies:
+                copy.wait_send()
 
     for copy in first:
         copy.wait_send()
@@ -312,7 +335,7 @@
 
 def local(embeddings, centroids, block_lists, block_counts):
     vmem = pl.BlockSpec(memory_space=pltpu.VMEM)
-    copies = ITERS * COPIES
+    copies = ITERS * COPIES * 2
     swaps = (ITERS + 1) * PIECES
     current, evidence = pl.pallas_call(
         kernel,

time: 95.1 us -> 90.9 us (0.956); the launches traced: 93.5 us -> 90.7 us
  Pallas kernels: 88.5 us -> 85.7 us
    pallas_call x1, Pallas kernels: 88.5 us -> 85.7 us  [local(): pl.pallas_call(kernel, out_shape=(jax.ShapeDtypeStruct((CB, HALF), jnp.fl...]
where the time goes in v4:
time: 90.9 us; the launch traced here: 90.7 us
  Pallas kernels  85.7 us (94%)
  local copies, waits for them, and re-layouts  3.04 us (3%)
  other arithmetic  1.31 us (1%)
    pallas_call x1, Pallas kernels, local(): pl.pallas_call(kernel, out_shape=(jax.ShapeDtypeStruct((CB, HALF), jnp.fl...  85.7 us
    unnamed x2, local copies, waits for them, and re-layouts  3.04 us

profile of v4, /device:TPU:1, one launch (start us, length us, event | category | flops | bytes accessed | tf_op | source)
XLA Modules:
  0.0 90.7 jit_solution(17462180964955130449)
XLA Ops:
  0.6 1.4 %copy.6.lists = s32[12,7]{1,0:T(8,128)} copy(s32[12,7]{0,1:T(8,128)} %param.6) | data formatting | bytes 672 | tf_op args[2]
  2.0 85.7 %kmeans.1 = (f32[128,512]{1,0:T(8,128)}, f32[1,1536]{1,0:T(1,128)}) custom-call(bf16[1536,1024]{1,0:T(8,128)(2,1)} %emb.1, f32[128,512]{1,0:T(8,128)} %cent.1, s32[12,7]{1,0:T(8,128)} %copy.6.lists, s32[12]{0:T(128)} %counts.1), custom_call_target="tpu_custom_call" | custom-call | tf_op jit(solution)/shard_map/kmeans/pallas_call | solution.py:340
  87.7 1.3 %reduce = f32[1536]{0:T(1024)} reduce(f32[1,1536]{1,0:T(1,128)} %get-tuple-element.5, f32[]{:T(128)} %constant.2), dimensions={0}, to_apply=%get-tuple-element.5.reduce_sub_computation | reduce | bytes 12292 | tf_op jit(solution)/shard_map/kmeans/pallas_call | solution.py:340
  89.0 1.7 %copy.8 = f32[128,512]{1,0:T(8,128)} copy(f32[128,512]{1,0:T(8,128)} %get-tuple-element.8) | data formatting | bytes 524288
